TPU v7x, 512 devices: a whole 4x8x8 slice. The times are simulated.
512 devices in a mesh: face: 16 (over x, z_hi, core), patch: 32 (over z_lo, y).
Axes of the slice: x: 4, y: 8, z: 8 (z_hi: 2, z_lo: 4; z = z_hi * 4 + z_lo), core: 2. Of those that a mesh axis runs over, the one named last changes fastest.
Arguments:
- dust_map: float32 [128, 32768], P('face', 'patch'), may hold values from -12 to 12
- seam_flags: int32 [16, 32, 4], P('face', 'patch'), may hold values from 0 to 1
- block_weights: int32 [128, 4096], P('face', 'patch'), may hold values from 1 to 4
Outputs:
- energy_field: float32 [128, 32768], P('face', 'patch')
- face_moments: float32 [16, 3, 128], P('face')
- sky_moments: float32 [3, 128], replicated
All inputs are finite; a program needn't handle non-finite values.
Results may differ from a plain program's by a relative error of at most 0.0003.
Values sent between devices are 32-bit elements; how exact they have to be, the bound alone decides.
No kernel may reach another device: no remote copies, remote signals or barrier semaphores. Data moves between devices by JAX's collectives and lax.ppermute only.
A program may use at most 64 MiB of HBM per device.

v0:
```python
import math
import jax
import jax.numpy as jnp
import numpy as np
from jax import lax
from jax.sharding import PartitionSpec as P

rim_depth = 4
epsilon = 1e-06
pair_list = ((0, 1), (0, 2), (1, 2))


def extended_2(cells, sides, width):
    for axis, dim in sides:
        count = lax.axis_size(axis)
        head = lax.slice_in_dim(cells, 0, width, axis=dim)
        tail = lax.slice_in_dim(cells, cells.shape[dim] - width, cells.shape[dim], axis=dim)
        cells = jnp.concatenate(
            [
                lax.ppermute(tail, axis, [(i, (i + 1) % count) for i in range(count)]),
                cells,
                lax.ppermute(head, axis, [((i + 1) % count, i) for i in range(count)]),
            ],
            axis=dim,
        )
    return cells


def filter_table():
    shift_rows = np.repeat(np.array([-1.0, 0.0, 1.0]), 3)
    shift_cols = np.tile(np.array([-1.0, 0.0, 1.0]), 3)
    envelope = np.exp(-(shift_rows**2 + shift_cols**2) / 1.28)
    real_rows = []
    imag_rows = []
    for orient in range(8):
        heading = math.pi * orient / 8.0
        phases = 2.2 * (shift_rows * math.cos(heading) + shift_cols * math.sin(heading))
        cosine_part = np.cos(phases) - np.sum(envelope * np.cos(phases)) / np.sum(envelope)
        sine_part = np.sin(phases) - np.sum(envelope * np.sin(phases)) / np.sum(envelope)
        norm_sq = np.sum(envelope**2 * (cosine_part**2 + sine_part**2))
        real_rows.append(envelope * cosine_part / np.sqrt(norm_sq))
        imag_rows.append(envelope * sine_part / np.sqrt(norm_sq))
    return np.stack(real_rows + imag_rows).astype(np.float32)


def turn_rims(extended, seam_bits):
    top_rim = extended[..., :rim_depth, rim_depth:-rim_depth]
    bottom_rim = extended[..., -rim_depth:, rim_depth:-rim_depth]
    left_rim = extended[..., rim_depth:-rim_depth, :rim_depth]
    right_rim = extended[..., rim_depth:-rim_depth, -rim_depth:]
    top_rim = jnp.where(seam_bits[0] > 0, jnp.flip(top_rim, -1), top_rim)
    bottom_rim = jnp.where(seam_bits[1] > 0, jnp.flip(bottom_rim, -1), bottom_rim)
    left_rim = jnp.where(seam_bits[2] > 0, jnp.flip(left_rim, -2), left_rim)
    right_rim = jnp.where(seam_bits[3] > 0, jnp.flip(right_rim, -2), right_rim)
    upper_band = jnp.concatenate(
        [extended[..., :rim_depth, :rim_depth], top_rim, extended[..., :rim_depth, -rim_depth:]],
        axis=-1,
    )
    middle_band = jnp.concatenate(
        [left_rim, extended[..., rim_depth:-rim_depth, rim_depth:-rim_depth], right_rim], axis=-1
    )
    lower_band = jnp.concatenate(
        [
            extended[..., -rim_depth:, :rim_depth],
            bottom_rim,
            extended[..., -rim_depth:, -rim_depth:],
        ],
        axis=-1,
    )
    return jnp.concatenate([upper_band, middle_band, lower_band], axis=-2)


def stencil(extended, dilation, tile_rows, tile_cols, filters):
    pieces = []
    for shift_row in (-1, 0, 1):
        for shift_col in (-1, 0, 1):
            first_row = rim_depth + shift_row * dilation
            first_col = rim_depth + shift_col * dilation
            pieces.append(
                extended[..., first_row : first_row + tile_rows, first_col : first_col + tile_cols]
            )
    stacked = jnp.stack(pieces, 0)
    return jnp.einsum("kt,t...->k...", filters, stacked, precision=lax.Precision.HIGHEST)


def first_layer(extended, tile_rows, tile_cols, filters):
    responses = jnp.stack(
        [stencil(extended, 2**octave, tile_rows, tile_cols, filters) for octave in range(3)]
    )
    moduli = jnp.sqrt(responses[:, :8] ** 2 + responses[:, 8:] ** 2 + epsilon)
    return (responses, moduli)


def second_layer(rimmed, responses, weights, scales, filters, tile_rows, tile_cols):
    moment_rows = []
    energy_parts = []
    for fine_level, coarse_level in pair_list:
        outputs = stencil(
            rimmed[8 * fine_level : 8 * fine_level + 8],
            2**coarse_level,
            tile_rows,
            tile_cols,
            filters,
        )
        outputs = outputs.reshape(2, 8, 8, tile_rows, tile_cols)
        coarse = (responses[coarse_level] * scales[coarse_level]).reshape(
            2, 8, tile_rows, tile_cols
        )
        squares = outputs * outputs
        third_order = jnp.einsum(
            "atrc,atsrc->st", coarse * weights, outputs, precision=lax.Precision.HIGHEST
        )
        fourth_order = jnp.einsum("atsrc,rc->st", squares, weights, precision=lax.Precision.HIGHEST)
        moment_rows.append(jnp.concatenate([third_order.reshape(64), fourth_order.reshape(64)]))
        energy_parts.append(jnp.sum(squares, axis=(0, 1, 2)))
    return (jnp.stack(moment_rows), jnp.stack(energy_parts))


def on_device(dust_map, seam_flags, block_weights):
    tile_rows, tile_cols = dust_map.shape
    filters = jnp.asarray(filter_table())
    seam_bits = seam_flags.reshape(4)
    repeat_by = tile_cols // block_weights.shape[1]
    weights = jnp.repeat(block_weights.astype(jnp.float32), repeat_by, axis=1)
    extended = extended_2(dust_map, (("face", 0), ("patch", 1)), 4)
    extended = turn_rims(extended, seam_bits)
    responses, moduli = first_layer(extended, tile_rows, tile_cols, filters)
    power_terms = jnp.einsum(
        "jtrc,rc->j", moduli * moduli, weights, precision=lax.Precision.HIGHEST
    )
    weight_total = jnp.sum(weights)
    power_sums, weight_sum = lax.psum((power_terms, weight_total), ("face", "patch"))
    levels = power_sums / (8.0 * weight_sum)
    scales = 1.0 / jnp.sqrt(levels)
    fields = (moduli[:2] * scales[:2, None, None, None]).reshape(16, tile_rows, tile_cols)
    rimmed = extended_2(fields, (("face", 1), ("patch", 2)), 4)
    rimmed = turn_rims(rimmed, seam_bits)
    moment_rows, energy_parts = second_layer(
        rimmed, responses, weights, scales, filters, tile_rows, tile_cols
    )
    face_raw, face_weight = lax.psum((moment_rows, weight_total), "patch")
    sky_raw = lax.psum(face_raw, "face")
    face_moments = face_raw / face_weight
    sky_moments = sky_raw / weight_sum
    energy = jnp.sum(energy_parts, 0) / 192.0
    return (energy, face_moments[None], sky_moments)


def solution(mesh):
    return jax.shard_map(
        on_device,
        mesh=mesh,
        in_specs=(P("face", "patch"), P("face", "patch", None), P("face", "patch")),
        out_specs=(P("face", "patch"), P("face", None, None), P()),
        check_vma=False,
    )
```

profile of v0, /device:TPU:1, one launch (start us, length us, event | category | flops | bytes accessed | tf_op | source)
XLA Modules:
  0.0 429.5 jit_solution(8411601705834357442)
XLA Ops:
  1.5 12.0 %collective-permute-start = (f32[4,1024]{1,0:T(4,128)S(1)}, f32[4,1024]{1,0:T(4,128)S(1)}, u32[]{:S(2)}, u32[]{:S(2)}) collective-permute-start(f32[4,1024]{1,0:T(4,128)S(1)} %get-tuple-element.74), channel_id=1, source_target_pairs={{0,32},{32,64},{64,96},{96,128},{128,160},{160,192},{192,224},{224... | collective-permute-start | bytes 49160 | tf_op jit(solution)/shard_map/ppermute | solution.py:20
  13.5 1.9 collective-permute-start.1
  17.0 1.4 fusion.145
  23.3 7.8 %collective-permute-start.3 = (f32[16,4]{1,0:T(8,128)S(1)}, f32[16,4]{1,0:T(8,128)S(1)}, u32[]{:S(2)}, u32[]{:S(2)}) collective-permute-start(f32[16,4]{1,0:T(8,128)S(1)} %get-tuple-element.51), channel_id=1, source_target_pairs={{1,0},{2,1},{3,2},{4,3},{5,4},{6,5},{7,6},{8,7},{9,8},{10,9},{11,1... | collective-permute-start | bytes 776 | tf_op jit(solution)/shard_map/ppermute | solution.py:22
  31.1 1.9 collective-permute-start.2
  34.5 4.9 %collective-permute-done.2 = f32[16,4]{1,0:T(8,128)S(1)} collective-permute-done((f32[16,4]{1,0:T(8,128)S(1)}, f32[16,4]{1,0:T(8,128)S(1)}, u32[]{:S(2)}, u32[]{:S(2)}) %collective-permute-start.2) | collective-permute-done | bytes 288 | tf_op jit(solution)/shard_map/ppermute | solution.py:20
  50.1 1.7 fusion.18
  51.9 1.3 multiply_reduce_fusion.6
  53.9 95.6 %all-reduce = (f32[3]{0:T(128)S(1)}, f32[]{:T(128)}) all-reduce(f32[3]{0:T(128)S(1)} %convolution_bitcast_fusion.1, f32[]{:T(128)} %broadcast_reduce_fusion), channel_id=1, replica_groups=mesh['face'=16,'patch'=32] {'face','patch'}, use_global_device_ids=true, to_apply=%region_1.2 | all-reduce | flops 4 | bytes 32 | tf_op jit(solution)/shard_map/psum | solution.py:132
  150.1 1.2 slice_multiply_fusion.2
  152.7 7.0 %collective-permute-start.4 = (f32[16,4,1024]{2,0,1:T(8,128)}, f32[16,4,1024]{2,0,1:T(8,128)S(1)}, u32[]{:S(2)}, u32[]{:S(2)}) collective-permute-start(f32[16,4,1024]{2,0,1:T(8,128)} %get-tuple-element.42), channel_id=1, source_target_pairs={{0,32},{32,64},{64,96},{96,128},{128,160},{160,192},{192,224},{224... | collective-permute-start | bytes 786440 | tf_op jit(solution)/shard_map/ppermute | solution.py:20
  160.8 1.9 collective-permute-start.5
  163.4 2.6 collective-permute-done.4
  168.6 4.1 collective-permute-done.5
  175.2 5.8 %collective-permute-start.7 = (f32[16,16,4]{2,0,1:T(8,128)S(1)}, f32[16,16,4]{2,0,1:T(8,128)S(1)}, u32[]{:S(2)}, u32[]{:S(2)}) collective-permute-start(f32[16,16,4]{2,0,1:T(8,128)S(1)} %get-tuple-element.18), channel_id=1, source_target_pairs={{1,0},{2,1},{3,2},{4,3},{5,4},{6,5},{7,6},{8,7},{9,8},{10,9},{11,1... | collective-permute-start | bytes 12296 | tf_op jit(solution)/shard_map/ppermute | solution.py:22
  181.0 2.4 fusion.16
  183.4 2.4 collective-permute-start.6
  185.8 8.3 %collective-permute-done.6 = f32[16,16,4]{2,0,1:T(8,128)S(1)} collective-permute-done((f32[16,16,4]{2,0,1:T(8,128)S(1)}, f32[16,16,4]{2,0,1:T(8,128)S(1)}, u32[]{:S(2)}, u32[]{:S(2)}) %collective-permute-start.6) | collective-permute-done | bytes 4128 | tf_op jit(solution)/shard_map/ppermute | solution.py:20
  196.1 1.4 copy-done.1
  204.5 5.5 %multiply_reduce_fusion.4 = (f32[8,1024]{1,0:T(8,128)}, f32[16,8,8,1024]{3,0,2,1:T(8,128)S(1)}) fusion(f32[16,9,1,1]{1,0,3,2:T(8,128)S(1)} %copy-done.12, f32[9,8,8,1024]{3,1,2,0:T(8,128)S(1)} %get-tuple-element.20), kind=kOutput, calls=%fused_computation.16 | convolution fusion | flops 115335168 | bytes 6586944 | tf_op jit(solution)/shard_map/kt,t...->k.../dot_general | solution.py:83
  211.0 11.9 %fusion.2 = f32[8,1,8,1,1]{2,1,4,3,0:T(1,128)S(1)} fusion(f32[2,8,8,8,1024]{4,1,0,3,2:T(8,128)S(1)} %bitcast.261, f32[2,8,8,1024,1]{3,1,0,2,4:T(8,128)S(1)} %copy-done.4), kind=kOutput, calls=%fused_computation.2 | convolution fusion | flops 12582912 | bytes 4718848 | tf_op jit(solution)/shard_map/atrc,atsrc->st/dot_general | solution.py:110
  223.0 13.9 %fusion.147 = f32[1,8,8,1]{1,0,3,2:T(1,128)S(1)} fusion(f32[8,8,8,1024]{3,0,2,1:T(8,128)S(1)} %multiply_reduce_fusion.1, f32[8,1024,1,1]{1,2,0,3:T(1,128)S(1)} %copy-done.9), kind=kOutput, calls=%fused_computation.293 | convolution fusion | flops 6291456 | bytes 2130176 | tf_op jit(solution)/shard_map/atsrc,rc->st/dot_general | solution.py:113
  239.0 6.7 %multiply_reduce_fusion.5 = (f32[8,1024]{1,0:T(8,128)S(1)}, f32[16,8,8,1024]{3,0,2,1:T(8,128)S(1)}) fusion(f32[16,9,1,1]{1,0,3,2:T(8,128)S(1)} %copy-done.12, f32[9,8,8,1024]{3,1,2,0:T(8,128)} %get-tuple-element.26), kind=kOutput, calls=%fused_computation.17 | convolution fusion | flops 115335168 | bytes 6586944 | tf_op jit(solution)/shard_map/kt,t...->k.../dot_general | solution.py:83
  245.7 1.8 multiply_reduce_fusion.2
  247.5 12.1 %fusion.4 = f32[8,1,8,1,1]{2,1,4,3,0:T(1,128)S(1)} fusion(f32[2,8,8,8,1024]{4,1,0,3,2:T(8,128)S(1)} %bitcast.259, f32[2,8,8,1024,1]{3,1,0,2,4:T(8,128)S(1)} %copy-done.7), kind=kOutput, calls=%fused_computation.4 | convolution fusion | flops 12582912 | bytes 4718848 | tf_op jit(solution)/shard_map/atrc,atsrc->st/dot_general | solution.py:110
  259.8 4.8 %multiply_reduce_fusion.3 = (f32[8,1024]{1,0:T(8,128)S(1)}, f32[16,8,8,1024]{3,0,2,1:T(8,128)S(1)}) fusion(f32[16,9,1,1]{1,0,3,2:T(8,128)S(1)} %copy-done.12, f32[9,8,8,1024]{3,1,2,0:T(8,128)S(1)} %copy-done), kind=kOutput, calls=%fused_computation.15 | convolution fusion | flops 115335168 | bytes 6586944 | tf_op jit(solution)/shard_map/kt,t...->k.../dot_general | solution.py:83
  264.6 1.8 multiply_reduce_fusion
  266.4 11.9 %fusion = f32[8,1,8,1,1]{2,1,4,3,0:T(1,128)S(1)} fusion(f32[2,8,8,8,1024]{4,1,0,3,2:T(8,128)S(1)} %bitcast.260, f32[2,8,8,1024,1]{3,1,0,2,4:T(8,128)S(1)} %copy-done.5), kind=kOutput, calls=%fused_computation | convolution fusion | flops 12582912 | bytes 4718848 | tf_op jit(solution)/shard_map/atrc,atsrc->st/dot_general | solution.py:110
  278.4 15.5 %fusion.148 = f32[1,8,8,1]{1,0,3,2:T(1,128)S(1)} fusion(f32[8,8,8,1024]{3,0,2,1:T(8,128)} %multiply_reduce_fusion, f32[8,1024,1,1]{1,2,0,3:T(1,128)S(1)} %copy-done.9), kind=kOutput, calls=%fused_computation.294 | convolution fusion | flops 6291456 | bytes 2130176 | tf_op jit(solution)/shard_map/atsrc,rc->st/dot_general | solution.py:113
  294.0 14.1 %fusion.146 = f32[1,8,8,1]{1,0,3,2:T(1,128)S(1)} fusion(f32[8,8,8,1024]{3,0,2,1:T(8,128)S(1)} %copy-done.3, f32[8,1024,1,1]{1,2,0,3:T(1,128)S(1)} %copy-done.9), kind=kOutput, calls=%fused_computation.292 | convolution fusion | flops 6291456 | bytes 2130176 | tf_op jit(solution)/shard_map/atsrc,rc->st/dot_general | solution.py:113
  308.3 61.2 %all-reduce.1 = (f32[3,128]{1,0:T(4,128)S(1)}, f32[]{:T(128)}) all-reduce(f32[3,128]{1,0:T(4,128)S(1)} %pad_maximum_fusion.12, f32[]{:T(128)} %broadcast_reduce_fusion), channel_id=1, replica_groups=mesh['face'=16,'patch'=32] {'patch'}, use_global_device_ids=true, to_apply=%region_10.11 | all-reduce | flops 385 | bytes 3080 | tf_op jit(solution)/shard_map/psum | solution.py:141
  369.6 56.7 %psum.39 = f32[3,128]{1,0:T(4,128)S(1)} all-reduce(f32[3,128]{1,0:T(4,128)S(1)} %get-tuple-element.14), channel_id=1, replica_groups=mesh['face'=16,'patch'=32] {'face'}, use_global_device_ids=true, to_apply=%region_12.13 | all-reduce | flops 384 | bytes 3072 | tf_op jit(solution)/shard_map/psum | solution.py:142
  (136 shorter events, 41.7 us)
Async XLA Ops:
  0.6 46.1 %copy-start.13 = (f32[16,9,1]{1,0,2:T(8,128)S(1)}, f32[16,9,1]{1,0,2:T(8,128)}, u32[]{:S(2)}) copy-start(f32[16,9,1]{1,0,2:T(8,128)} %constant.23) | copy-start | bytes 1732
  0.6 42.1 %copy-start.6 = (f32[8,1024]{1,0:T(8,128)S(1)}, f32[8,1024]{1,0:T(8,128)}, u32[]{:S(2)}) copy-start(f32[8,1024]{1,0:T(8,128)} %param.4) | copy-start | bytes 98308
  1.5 20.8 %collective-permute-start = (f32[4,1024]{1,0:T(4,128)S(1)}, f32[4,1024]{1,0:T(4,128)S(1)}, u32[]{:S(2)}, u32[]{:S(2)}) collective-permute-start(f32[4,1024]{1,0:T(4,128)S(1)} %get-tuple-element.74), channel_id=1, source_target_pairs={{0,32},{32,64},{64,96},{96,128},{128,160},{160,192},{192,224},{224... | collective-permute-start | bytes 49160 | tf_op jit(solution)/shard_map/ppermute | solution.py:20
  13.5 9.0 %collective-permute-start.1 = (f32[4,1024]{1,0:T(4,128)S(1)}, f32[4,1024]{1,0:T(4,128)S(1)}, u32[]{:S(2)}, u32[]{:S(2)}) collective-permute-start(f32[4,1024]{1,0:T(4,128)S(1)} %get-tuple-element.75), channel_id=1, source_target_pairs={{32,0},{64,32},{96,64},{128,96},{160,128},{192,160},{224,192},{256... | collective-permute-start | bytes 49160 | tf_op jit(solution)/shard_map/ppermute | solution.py:22
  23.3 11.2 %collective-permute-start.3 = (f32[16,4]{1,0:T(8,128)S(1)}, f32[16,4]{1,0:T(8,128)S(1)}, u32[]{:S(2)}, u32[]{:S(2)}) collective-permute-start(f32[16,4]{1,0:T(8,128)S(1)} %get-tuple-element.51), channel_id=1, source_target_pairs={{1,0},{2,1},{3,2},{4,3},{5,4},{6,5},{7,6},{8,7},{9,8},{10,9},{11,1... | collective-permute-start | bytes 776 | tf_op jit(solution)/shard_map/ppermute | solution.py:22
  31.1 8.3 %collective-permute-start.2 = (f32[16,4]{1,0:T(8,128)S(1)}, f32[16,4]{1,0:T(8,128)S(1)}, u32[]{:S(2)}, u32[]{:S(2)}) collective-permute-start(f32[16,4]{1,0:T(8,128)S(1)} %get-tuple-element.52), channel_id=1, source_target_pairs={{0,1},{1,2},{2,3},{3,4},{4,5},{5,6},{6,7},{7,8},{8,9},{9,10},{10,1... | collective-permute-start | bytes 776 | tf_op jit(solution)/shard_map/ppermute | solution.py:20
  152.7 13.2 %collective-permute-start.4 = (f32[16,4,1024]{2,0,1:T(8,128)}, f32[16,4,1024]{2,0,1:T(8,128)S(1)}, u32[]{:S(2)}, u32[]{:S(2)}) collective-permute-start(f32[16,4,1024]{2,0,1:T(8,128)} %get-tuple-element.42), channel_id=1, source_target_pairs={{0,32},{32,64},{64,96},{96,128},{128,160},{160,192},{192,224},{224... | collective-permute-start | bytes 786440 | tf_op jit(solution)/shard_map/ppermute | solution.py:20
  160.8 11.9 %collective-permute-start.5 = (f32[16,4,1024]{2,0,1:T(8,128)}, f32[16,4,1024]{2,0,1:T(8,128)S(1)}, u32[]{:S(2)}, u32[]{:S(2)}) collective-permute-start(f32[16,4,1024]{2,0,1:T(8,128)} %get-tuple-element.41), channel_id=1, source_target_pairs={{32,0},{64,32},{96,64},{128,96},{160,128},{192,160},{224,192},{256... | collective-permute-start | bytes 786440 | tf_op jit(solution)/shard_map/ppermute | solution.py:22
  167.6 1.0 copy-start.10
  174.1 20.4 %copy-start.8 = (f32[16,4,1024]{2,0,1:T(8,128)S(1)}, f32[16,4,1024]{2,0,1:T(8,128)}, u32[]{:S(2)}) copy-start(f32[16,4,1024]{2,0,1:T(8,128)} %get-tuple-element.45) | copy-start | bytes 786436
  175.2 10.5 %collective-permute-start.7 = (f32[16,16,4]{2,0,1:T(8,128)S(1)}, f32[16,16,4]{2,0,1:T(8,128)S(1)}, u32[]{:S(2)}, u32[]{:S(2)}) collective-permute-start(f32[16,16,4]{2,0,1:T(8,128)S(1)} %get-tuple-element.18), channel_id=1, source_target_pairs={{1,0},{2,1},{3,2},{4,3},{5,4},{6,5},{7,6},{8,7},{9,8},{10,9},{11,1... | collective-permute-start | bytes 12296 | tf_op jit(solution)/shard_map/ppermute | solution.py:22
  183.4 10.7 %collective-permute-start.6 = (f32[16,16,4]{2,0,1:T(8,128)S(1)}, f32[16,16,4]{2,0,1:T(8,128)S(1)}, u32[]{:S(2)}, u32[]{:S(2)}) collective-permute-start(f32[16,16,4]{2,0,1:T(8,128)S(1)} %get-tuple-element.19), channel_id=1, source_target_pairs={{0,1},{1,2},{2,3},{3,4},{4,5},{5,6},{6,7},{7,8},{8,9},{9,10},{10,1... | collective-permute-start | bytes 12296 | tf_op jit(solution)/shard_map/ppermute | solution.py:20
  196.1 1.4 copy-start.1
  199.6 3.9 copy-start.2
  200.7 3.8 copy-start.12
  210.0 1.0 copy-start.4
  211.0 12.0 %copy-start.9 = (f32[8,1024,1,1]{1,2,0,3:T(1,128)S(1)}, f32[8,1024,1,1]{1,2,0,3:T(1,128)}, u32[]{:S(2)}) copy-start(f32[8,1024,1,1]{1,2,0,3:T(1,128)} %reshape.101) | copy-start | bytes 98308
  245.7 1.8 copy-start.7
  247.5 12.2 %copy-start = (f32[9,8,8,1024]{3,1,2,0:T(8,128)S(1)}, f32[9,8,8,1024]{3,1,2,0:T(8,128)}, u32[]{:S(2)}) copy-start(f32[9,8,8,1024]{3,1,2,0:T(8,128)} %get-tuple-element.27) | copy-start | bytes 7077892
  264.6 1.8 copy-start.5
  266.4 27.6 %copy-start.3 = (f32[8,8,8,1024]{3,0,2,1:T(8,128)S(1)}, f32[8,8,8,1024]{3,0,2,1:T(8,128)}, u32[]{:S(2)}) copy-start(f32[8,8,8,1024]{3,0,2,1:T(8,128)} %multiply_reduce_fusion.2) | copy-start | bytes 6291460
  278.3 150.3 %copy-start.11 = (f32[8,1024]{1,0:T(8,128)S(1)}, f32[8,1024]{1,0:T(8,128)}, u32[]{:S(2)}) copy-start(f32[8,1024]{1,0:T(8,128)} %get-tuple-element.90) | copy-start | bytes 98308
where the time goes:
time: 437 us; the launch traced here: 429 us
  blocking collectives  214 us (49%)
  matrix products  99.8 us (23%)
  starting transfers between devices  40.7 us (9%)
  other arithmetic  31.7 us (7%)
  waiting for transfers between devices  20.1 us (5%)
  local copies, waits for them, and re-layouts  19.1 us (4%)
  between operations  4.59 us (1%)
    psum x1, blocking collectives, on_device(): lax.psum((power_terms, weight_total), ('face', 'patch'))  95.6 us
    psum x1, blocking collectives, on_device(): face_raw, face_weight = lax.psum((moment_rows, weight_total), 'patch')  61.2 us
    psum x1, blocking collectives, on_device(): sky_raw = lax.psum(face_raw, 'face')  56.7 us
    dot_general x3, matrix products, second_layer(): jnp.einsum('atsrc,rc->st', squares, weights, precision=lax.Precision.HIGH...  43.4 us
    dot_general x3, matrix products, second_layer(): jnp.einsum('atrc,atsrc->st', coarse * weights, outputs, precision=lax.Pre...  35.8 us
    ppermute x4, starting transfers between devices, extended_2(): lax.ppermute(tail, axis, [(i, (i + 1) % count) for i in range(count)])  23.2 us
    dot_general x6, matrix products, stencil(): jnp.einsum('kt,t...->k...', filters, stacked, precision=lax.Precision.HIG...  19.9 us
    ppermute x4, starting transfers between devices, extended_2(): lax.ppermute(head, axis, [((i + 1) % count, i) for i in range(count)])  17.4 us
  transfers between devices with their start and end apart: 8, of which 5 were waited for; matrix products, arithmetic and copies ran while one was open for 3% of the time, Pallas kernels for 0%

commit v1 on v0

--- a/solution.py
+++ b/solution.py
@@ -4,6 +4,7 @@
 import numpy as np
 from jax import lax
 from jax.sharding import PartitionSpec as P
+from jax.lax import all_gather
 
 rim_depth = 4
 epsilon = 1e-06
@@ -139,7 +140,7 @@
         rimmed, responses, weights, scales, filters, tile_rows, tile_cols
     )
     face_raw, face_weight = lax.psum((moment_rows, weight_total), "patch")
-    sky_raw = lax.psum(face_raw, "face")
+    sky_raw = all_gather(face_raw, "face").sum(axis=0)
     face_moments = face_raw / face_weight
     sky_moments = sky_raw / weight_sum
     energy = jnp.sum(energy_parts, 0) / 192.0

time: 437 us -> 420 us (0.961)
  blocking collectives: 214 us -> 197 us
    psum x1 -> x0, blocking collectives: 56.7 us -> none  [on_device(): sky_raw = lax.psum(face_raw, 'face')]
    all_gather x0 -> x1, blocking collectives: none -> 39.7 us  [on_device(): sky_raw = all_gather(face_raw, 'face').sum(axis=0)]
where the time goes in v1:
time: 420 us; the launch traced here: 413 us
  blocking collectives  197 us (47%)
  matrix products  99.8 us (24%)
  starting transfers between devices  40.7 us (10%)
  other arithmetic  31.7 us (8%)
  waiting for transfers between devices  20.1 us (5%)
  local copies, waits for them, and re-layouts  19.1 us (5%)
  between operations  4.59 us (1%)
    psum x1, blocking collectives, on_device(): lax.psum((power_terms, weight_total), ('face', 'patch'))  95.6 us
    psum x1, blocking collectives, on_device(): face_raw, face_weight = lax.psum((moment_rows, weight_total), 'patch')  61.2 us
    dot_general x3, matrix products, second_layer(): jnp.einsum('atsrc,rc->st', squares, weights, precision=lax.Precision.HIGH...  43.4 us
    all_gather x1, blocking collectives, on_device(): sky_raw = all_gather(face_raw, 'face').sum(axis=0)  39.7 us
    dot_general x3, matrix products, second_layer(): jnp.einsum('atrc,atsrc->st', coarse * weights, outputs, precision=lax.Pre...  35.8 us
    ppermute x4, starting transfers between devices, extended_2(): lax.ppermute(tail, axis, [(i, (i + 1) % count) for i in range(count)])  23.2 us
    dot_general x6, matrix products, stencil(): jnp.einsum('kt,t...->k...', filters, stacked, precision=lax.Precision.HIG...  19.9 us
    ppermute x4, starting transfers between devices, extended_2(): lax.ppermute(head, axis, [((i + 1) % count, i) for i in range(count)])  17.4 us
  transfers between devices with their start and end apart: 8, of which 5 were waited for; matrix products, arithmetic and copies ran while one was open for 3% of the time, Pallas kernels for 0%

profile of v1, /device:TPU:1, one launch (start us, length us, event | category | flops | bytes accessed | tf_op | source)
XLA Modules:
  0.0 412.5 jit_solution(585193986728215941)
XLA Ops:
  1.5 12.0 %collective-permute-start = (f32[4,1024]{1,0:T(4,128)S(1)}, f32[4,1024]{1,0:T(4,128)S(1)}, u32[]{:S(2)}, u32[]{:S(2)}) collective-permute-start(f32[4,1024]{1,0:T(4,128)S(1)} %get-tuple-element.74), channel_id=1, source_target_pairs={{0,32},{32,64},{64,96},{96,128},{128,160},{160,192},{192,224},{224... | collective-permute-start | bytes 49160 | tf_op jit(solution)/shard_map/ppermute | solution.py:21
  13.5 1.9 collective-permute-start.1
  17.0 1.4 fusion.145
  23.3 7.8 %collective-permute-start.3 = (f32[16,4]{1,0:T(8,128)S(1)}, f32[16,4]{1,0:T(8,128)S(1)}, u32[]{:S(2)}, u32[]{:S(2)}) collective-permute-start(f32[16,4]{1,0:T(8,128)S(1)} %get-tuple-element.51), channel_id=1, source_target_pairs={{1,0},{2,1},{3,2},{4,3},{5,4},{6,5},{7,6},{8,7},{9,8},{10,9},{11,1... | collective-permute-start | bytes 776 | tf_op jit(solution)/shard_map/ppermute | solution.py:23
  31.1 1.9 collective-permute-start.2
  34.5 4.9 %collective-permute-done.2 = f32[16,4]{1,0:T(8,128)S(1)} collective-permute-done((f32[16,4]{1,0:T(8,128)S(1)}, f32[16,4]{1,0:T(8,128)S(1)}, u32[]{:S(2)}, u32[]{:S(2)}) %collective-permute-start.2) | collective-permute-done | bytes 288 | tf_op jit(solution)/shard_map/ppermute | solution.py:21
  50.1 1.7 fusion.18
  51.9 1.3 multiply_reduce_fusion.6
  53.9 95.6 %all-reduce = (f32[3]{0:T(128)S(1)}, f32[]{:T(128)}) all-reduce(f32[3]{0:T(128)S(1)} %convolution_bitcast_fusion.1, f32[]{:T(128)} %broadcast_reduce_fusion), channel_id=1, replica_groups=mesh['face'=16,'patch'=32] {'face','patch'}, use_global_device_ids=true, to_apply=%region_1.2 | all-reduce | flops 4 | bytes 32 | tf_op jit(solution)/shard_map/psum | solution.py:133
  150.1 1.2 slice_multiply_fusion.2
  152.7 7.0 %collective-permute-start.4 = (f32[16,4,1024]{2,0,1:T(8,128)}, f32[16,4,1024]{2,0,1:T(8,128)S(1)}, u32[]{:S(2)}, u32[]{:S(2)}) collective-permute-start(f32[16,4,1024]{2,0,1:T(8,128)} %get-tuple-element.42), channel_id=1, source_target_pairs={{0,32},{32,64},{64,96},{96,128},{128,160},{160,192},{192,224},{224... | collective-permute-start | bytes 786440 | tf_op jit(solution)/shard_map/ppermute | solution.py:21
  160.8 1.9 collective-permute-start.5
  163.4 2.6 collective-permute-done.4
  168.6 4.1 collective-permute-done.5
  175.2 5.8 %collective-permute-start.7 = (f32[16,16,4]{2,0,1:T(8,128)S(1)}, f32[16,16,4]{2,0,1:T(8,128)S(1)}, u32[]{:S(2)}, u32[]{:S(2)}) collective-permute-start(f32[16,16,4]{2,0,1:T(8,128)S(1)} %get-tuple-element.18), channel_id=1, source_target_pairs={{1,0},{2,1},{3,2},{4,3},{5,4},{6,5},{7,6},{8,7},{9,8},{10,9},{11,1... | collective-permute-start | bytes 12296 | tf_op jit(solution)/shard_map/ppermute | solution.py:23
  181.0 2.4 fusion.16
  183.4 2.4 collective-permute-start.6
  185.8 8.3 %collective-permute-done.6 = f32[16,16,4]{2,0,1:T(8,128)S(1)} collective-permute-done((f32[16,16,4]{2,0,1:T(8,128)S(1)}, f32[16,16,4]{2,0,1:T(8,128)S(1)}, u32[]{:S(2)}, u32[]{:S(2)}) %collective-permute-start.6) | collective-permute-done | bytes 4128 | tf_op jit(solution)/shard_map/ppermute | solution.py:21
  196.1 1.4 copy-done.1
  204.5 5.5 %multiply_reduce_fusion.4 = (f32[8,1024]{1,0:T(8,128)}, f32[16,8,8,1024]{3,0,2,1:T(8,128)S(1)}) fusion(f32[16,9,1,1]{1,0,3,2:T(8,128)S(1)} %copy-done.12, f32[9,8,8,1024]{3,1,2,0:T(8,128)S(1)} %get-tuple-element.20), kind=kOutput, calls=%fused_computation.16 | convolution fusion | flops 115335168 | bytes 6586944 | tf_op jit(solution)/shard_map/kt,t...->k.../dot_general | solution.py:84
  211.0 11.9 %fusion.2 = f32[8,1,8,1,1]{2,1,4,3,0:T(1,128)S(1)} fusion(f32[2,8,8,8,1024]{4,1,0,3,2:T(8,128)S(1)} %bitcast.262, f32[2,8,8,1024,1]{3,1,0,2,4:T(8,128)S(1)} %copy-done.4), kind=kOutput, calls=%fused_computation.2 | convolution fusion | flops 12582912 | bytes 4718848 | tf_op jit(solution)/shard_map/atrc,atsrc->st/dot_general | solution.py:111
  223.0 13.9 %fusion.147 = f32[1,8,8,1]{1,0,3,2:T(1,128)S(1)} fusion(f32[8,8,8,1024]{3,0,2,1:T(8,128)S(1)} %multiply_reduce_fusion.1, f32[8,1024,1,1]{1,2,0,3:T(1,128)S(1)} %copy-done.9), kind=kOutput, calls=%fused_computation.293 | convolution fusion | flops 6291456 | bytes 2130176 | tf_op jit(solution)/shard_map/atsrc,rc->st/dot_general | solution.py:114
  239.0 6.7 %multiply_reduce_fusion.5 = (f32[8,1024]{1,0:T(8,128)S(1)}, f32[16,8,8,1024]{3,0,2,1:T(8,128)S(1)}) fusion(f32[16,9,1,1]{1,0,3,2:T(8,128)S(1)} %copy-done.12, f32[9,8,8,1024]{3,1,2,0:T(8,128)} %get-tuple-element.26), kind=kOutput, calls=%fused_computation.17 | convolution fusion | flops 115335168 | bytes 6586944 | tf_op jit(solution)/shard_map/kt,t...->k.../dot_general | solution.py:84
  245.7 1.8 multiply_reduce_fusion.2
  247.5 12.1 %fusion.4 = f32[8,1,8,1,1]{2,1,4,3,0:T(1,128)S(1)} fusion(f32[2,8,8,8,1024]{4,1,0,3,2:T(8,128)S(1)} %bitcast.260, f32[2,8,8,1024,1]{3,1,0,2,4:T(8,128)S(1)} %copy-done.7), kind=kOutput, calls=%fused_computation.4 | convolution fusion | flops 12582912 | bytes 4718848 | tf_op jit(solution)/shard_map/atrc,atsrc->st/dot_general | solution.py:111
  259.8 4.8 %multiply_reduce_fusion.3 = (f32[8,1024]{1,0:T(8,128)S(1)}, f32[16,8,8,1024]{3,0,2,1:T(8,128)S(1)}) fusion(f32[16,9,1,1]{1,0,3,2:T(8,128)S(1)} %copy-done.12, f32[9,8,8,1024]{3,1,2,0:T(8,128)S(1)} %copy-done), kind=kOutput, calls=%fused_computation.15 | convolution fusion | flops 115335168 | bytes 6586944 | tf_op jit(solution)/shard_map/kt,t...->k.../dot_general | solution.py:84
  264.6 1.8 multiply_reduce_fusion
  266.4 11.9 %fusion = f32[8,1,8,1,1]{2,1,4,3,0:T(1,128)S(1)} fusion(f32[2,8,8,8,1024]{4,1,0,3,2:T(8,128)S(1)} %bitcast.261, f32[2,8,8,1024,1]{3,1,0,2,4:T(8,128)S(1)} %copy-done.5), kind=kOutput, calls=%fused_computation | convolution fusion | flops 12582912 | bytes 4718848 | tf_op jit(solution)/shard_map/atrc,atsrc->st/dot_general | solution.py:111
  278.4 15.5 %fusion.148 = f32[1,8,8,1]{1,0,3,2:T(1,128)S(1)} fusion(f32[8,8,8,1024]{3,0,2,1:T(8,128)} %multiply_reduce_fusion, f32[8,1024,1,1]{1,2,0,3:T(1,128)S(1)} %copy-done.9), kind=kOutput, calls=%fused_computation.294 | convolution fusion | flops 6291456 | bytes 2130176 | tf_op jit(solution)/shard_map/atsrc,rc->st/dot_general | solution.py:114
  294.0 14.1 %fusion.146 = f32[1,8,8,1]{1,0,3,2:T(1,128)S(1)} fusion(f32[8,8,8,1024]{3,0,2,1:T(8,128)S(1)} %copy-done.3, f32[8,1024,1,1]{1,2,0,3:T(1,128)S(1)} %copy-done.9), kind=kOutput, calls=%fused_computation.292 | convolution fusion | flops 6291456 | bytes 2130176 | tf_op jit(solution)/shard_map/atsrc,rc->st/dot_general | solution.py:114
  308.3 61.2 %all-reduce.1 = (f32[3,128]{1,0:T(4,128)S(1)}, f32[]{:T(128)}) all-reduce(f32[3,128]{1,0:T(4,128)S(1)} %pad_maximum_fusion.12, f32[]{:T(128)} %broadcast_reduce_fusion), channel_id=1, replica_groups=mesh['face'=16,'patch'=32] {'patch'}, use_global_device_ids=true, to_apply=%region_10.11 | all-reduce | flops 385 | bytes 3080 | tf_op jit(solution)/shard_map/psum | solution.py:142
  370.8 39.7 %all-gather.1 = f32[16,3,128]{2,1,0:T(4,128)S(1)} all-gather(f32[1,3,128]{2,1,0:T(4,128)S(1)} %bitcast.274), channel_id=2, replica_groups=mesh['face'=16,'patch'=32] {'face'}, dimensions={0}, use_global_device_ids=true | all-gather | bytes 26112 | tf_op jit(solution)/shard_map/all_gather | solution.py:143
  (137 shorter events, 41.7 us)
Async XLA Ops:
  0.6 46.1 %copy-start.13 = (f32[16,9,1]{1,0,2:T(8,128)S(1)}, f32[16,9,1]{1,0,2:T(8,128)}, u32[]{:S(2)}) copy-start(f32[16,9,1]{1,0,2:T(8,128)} %constant.23) | copy-start | bytes 1732
  0.6 42.1 %copy-start.6 = (f32[8,1024]{1,0:T(8,128)S(1)}, f32[8,1024]{1,0:T(8,128)}, u32[]{:S(2)}) copy-start(f32[8,1024]{1,0:T(8,128)} %param.4) | copy-start | bytes 98308
  1.5 20.8 %collective-permute-start = (f32[4,1024]{1,0:T(4,128)S(1)}, f32[4,1024]{1,0:T(4,128)S(1)}, u32[]{:S(2)}, u32[]{:S(2)}) collective-permute-start(f32[4,1024]{1,0:T(4,128)S(1)} %get-tuple-element.74), channel_id=1, source_target_pairs={{0,32},{32,64},{64,96},{96,128},{128,160},{160,192},{192,224},{224... | collective-permute-start | bytes 49160 | tf_op jit(solution)/shard_map/ppermute | solution.py:21
  13.5 9.0 %collective-permute-start.1 = (f32[4,1024]{1,0:T(4,128)S(1)}, f32[4,1024]{1,0:T(4,128)S(1)}, u32[]{:S(2)}, u32[]{:S(2)}) collective-permute-start(f32[4,1024]{1,0:T(4,128)S(1)} %get-tuple-element.75), channel_id=1, source_target_pairs={{32,0},{64,32},{96,64},{128,96},{160,128},{192,160},{224,192},{256... | collective-permute-start | bytes 49160 | tf_op jit(solution)/shard_map/ppermute | solution.py:23
  23.3 11.2 %collective-permute-start.3 = (f32[16,4]{1,0:T(8,128)S(1)}, f32[16,4]{1,0:T(8,128)S(1)}, u32[]{:S(2)}, u32[]{:S(2)}) collective-permute-start(f32[16,4]{1,0:T(8,128)S(1)} %get-tuple-element.51), channel_id=1, source_target_pairs={{1,0},{2,1},{3,2},{4,3},{5,4},{6,5},{7,6},{8,7},{9,8},{10,9},{11,1... | collective-permute-start | bytes 776 | tf_op jit(solution)/shard_map/ppermute | solution.py:23
  31.1 8.3 %collective-permute-start.2 = (f32[16,4]{1,0:T(8,128)S(1)}, f32[16,4]{1,0:T(8,128)S(1)}, u32[]{:S(2)}, u32[]{:S(2)}) collective-permute-start(f32[16,4]{1,0:T(8,128)S(1)} %get-tuple-element.52), channel_id=1, source_target_pairs={{0,1},{1,2},{2,3},{3,4},{4,5},{5,6},{6,7},{7,8},{8,9},{9,10},{10,1... | collective-permute-start | bytes 776 | tf_op jit(solution)/shard_map/ppermute | solution.py:21
  152.7 13.2 %collective-permute-start.4 = (f32[16,4,1024]{2,0,1:T(8,128)}, f32[16,4,1024]{2,0,1:T(8,128)S(1)}, u32[]{:S(2)}, u32[]{:S(2)}) collective-permute-start(f32[16,4,1024]{2,0,1:T(8,128)} %get-tuple-element.42), channel_id=1, source_target_pairs={{0,32},{32,64},{64,96},{96,128},{128,160},{160,192},{192,224},{224... | collective-permute-start | bytes 786440 | tf_op jit(solution)/shard_map/ppermute | solution.py:21
  160.8 11.9 %collective-permute-start.5 = (f32[16,4,1024]{2,0,1:T(8,128)}, f32[16,4,1024]{2,0,1:T(8,128)S(1)}, u32[]{:S(2)}, u32[]{:S(2)}) collective-permute-start(f32[16,4,1024]{2,0,1:T(8,128)} %get-tuple-element.41), channel_id=1, source_target_pairs={{32,0},{64,32},{96,64},{128,96},{160,128},{192,160},{224,192},{256... | collective-permute-start | bytes 786440 | tf_op jit(solution)/shard_map/ppermute | solution.py:23
  167.6 1.0 copy-start.10
  174.1 20.4 %copy-start.8 = (f32[16,4,1024]{2,0,1:T(8,128)S(1)}, f32[16,4,1024]{2,0,1:T(8,128)}, u32[]{:S(2)}) copy-start(f32[16,4,1024]{2,0,1:T(8,128)} %get-tuple-element.45) | copy-start | bytes 786436
  175.2 10.5 %collective-permute-start.7 = (f32[16,16,4]{2,0,1:T(8,128)S(1)}, f32[16,16,4]{2,0,1:T(8,128)S(1)}, u32[]{:S(2)}, u32[]{:S(2)}) collective-permute-start(f32[16,16,4]{2,0,1:T(8,128)S(1)} %get-tuple-element.18), channel_id=1, source_target_pairs={{1,0},{2,1},{3,2},{4,3},{5,4},{6,5},{7,6},{8,7},{9,8},{10,9},{11,1... | collective-permute-start | bytes 12296 | tf_op jit(solution)/shard_map/ppermute | solution.py:23
  183.4 10.7 %collective-permute-start.6 = (f32[16,16,4]{2,0,1:T(8,128)S(1)}, f32[16,16,4]{2,0,1:T(8,128)S(1)}, u32[]{:S(2)}, u32[]{:S(2)}) collective-permute-start(f32[16,16,4]{2,0,1:T(8,128)S(1)} %get-tuple-element.19), channel_id=1, source_target_pairs={{0,1},{1,2},{2,3},{3,4},{4,5},{5,6},{6,7},{7,8},{8,9},{9,10},{10,1... | collective-permute-start | bytes 12296 | tf_op jit(solution)/shard_map/ppermute | solution.py:21
  196.1 1.4 copy-start.1
  199.6 3.9 copy-start.2
  200.7 3.8 copy-start.12
  210.0 1.0 copy-start.4
  211.0 12.0 %copy-start.9 = (f32[8,1024,1,1]{1,2,0,3:T(1,128)S(1)}, f32[8,1024,1,1]{1,2,0,3:T(1,128)}, u32[]{:S(2)}) copy-start(f32[8,1024,1,1]{1,2,0,3:T(1,128)} %reshape.105) | copy-start | bytes 98308
  245.7 1.8 copy-start.7
  247.5 12.2 %copy-start = (f32[9,8,8,1024]{3,1,2,0:T(8,128)S(1)}, f32[9,8,8,1024]{3,1,2,0:T(8,128)}, u32[]{:S(2)}) copy-start(f32[9,8,8,1024]{3,1,2,0:T(8,128)} %get-tuple-element.27) | copy-start | bytes 7077892
  264.6 1.8 copy-start.5
  266.4 27.6 %copy-start.3 = (f32[8,8,8,1024]{3,0,2,1:T(8,128)S(1)}, f32[8,8,8,1024]{3,0,2,1:T(8,128)}, u32[]{:S(2)}) copy-start(f32[8,8,8,1024]{3,0,2,1:T(8,128)} %multiply_reduce_fusion.2) | copy-start | bytes 6291460
  278.3 133.4 %copy-start.11 = (f32[8,1024]{1,0:T(8,128)S(1)}, f32[8,1024]{1,0:T(8,128)}, u32[]{:S(2)}) copy-start(f32[8,1024]{1,0:T(8,128)} %get-tuple-element.90) | copy-start | bytes 98308
